TPU v7x, 512 devices: a whole 4x8x8 slice. The times are simulated.
512 devices in a mesh: rep: 64 (over x, y, core), mp: 8 (over z).
Axes of the slice: x: 4, y: 8, z: 8, core: 2. Of those that a mesh axis runs over, the one named last changes fastest.
Arguments:
- tokens_in: bfloat16 [16384, 8192], P('rep', 'mp'), may hold values from -2100 to 2100
- norm_gain: bfloat16 [8192], P('mp'), may hold values from 0.5 to 1.5
- key_grad: bfloat16 [16384, 512], P('rep'), may hold values from -1 to 1
- error_in: float32 [64, 8192, 512], P('rep', 'mp'), may hold values from -6 to 6
- basis_init: float32 [512, 128], P('mp'), may hold values from -6 to 6
- weights_in: float32 [8, 1024, 512], P('mp', 'rep'), may hold values from -0.75 to 0.75
- momentum_in: float32 [8, 1024, 512], P('mp', 'rep'), may hold values from -1.5 to 1.5
Outputs:
- error_out: float32 [64, 8192, 512], P('rep', 'mp')
- weights_out: float32 [8, 1024, 512], P('mp', 'rep')
- momentum_out: float32 [8, 1024, 512], P('mp', 'rep')
All inputs are finite; a program needn't handle non-finite values.
Results may differ from a plain program's by a relative error of at most 0.0025.
Values sent between devices are 32-bit elements; how exact they have to be, the bound alone decides.
A program may use at most 64 MiB of HBM per device.

v0:
```python
import jax
import jax.numpy as jnp
from jax import lax
from jax.sharding import PartitionSpec as P

D = 8192
ITERS = 2


precise = lax.Precision.HIGHEST
epsilon = 1e-05
momentum_rate = 0.9
outer_rate = 0.7


def product(first, second):
    return jnp.dot(first, second, precision=precise, preferred_element_type=jnp.float32)


def inner_product(first, second):
    return lax.dot_general(
        first,
        second,
        (((0,), (0,)), ((), ())),
        precision=precise,
        preferred_element_type=jnp.float32,
    )


def outer_product(first, second):
    return lax.dot_general(
        first,
        second,
        (((1,), (1,)), ((), ())),
        precision=precise,
        preferred_element_type=jnp.float32,
    )


def right_solve(lower_factor, row_block):
    return jax.scipy.linalg.solve_triangular(lower_factor, row_block.T, lower=True).T


def on_device(tokens_in, norm_gain, key_grad, error_in, basis_init, weights_in, momentum_in):
    replicas = lax.axis_size("rep")
    widened = tokens_in.astype(jnp.float32)
    square_sums = lax.psum(jnp.sum(widened * widened, axis=1), "mp")
    mean_square = square_sums / D
    right_factor = lax.all_gather(basis_init, "mp", axis=0, tiled=True)
    normed = (
        widened * lax.rsqrt(mean_square + epsilon)[:, None] * norm_gain.astype(jnp.float32)[None, :]
    ).astype(jnp.bfloat16)
    weight_change = lax.dot_general(
        normed, key_grad, (((0,), (0,)), ((), ())), preferred_element_type=jnp.float32
    )
    merged = weight_change + error_in[0]
    orthonormal = jnp.zeros((merged.shape[0], basis_init.shape[1]), jnp.float32)
    for iteration in range(ITERS):
        left_factor = lax.psum(product(merged, right_factor), "rep") / replicas
        gram_matrix = lax.psum(inner_product(left_factor, left_factor), "mp")
        lower_factor = jnp.linalg.cholesky(gram_matrix)
        orthonormal = right_solve(lower_factor, left_factor)
        right_factor = lax.psum(inner_product(merged, orthonormal), ("rep", "mp")) / replicas
    approximant = outer_product(orthonormal, right_factor)
    error_out = (merged - approximant)[None]
    rows_each = weights_in.shape[1]
    start_row = lax.axis_index("rep") * rows_each
    own_rows = lax.dynamic_slice_in_dim(approximant, start_row, rows_each, 0)[None]
    momentum_out = momentum_rate * momentum_in + own_rows
    weights_out = weights_in - outer_rate * (own_rows + momentum_rate * momentum_out)
    return (error_out, weights_out, momentum_out)


def solution(mesh):
    in_specs = (
        P("rep", "mp"),
        P("mp"),
        P("rep", None),
        P("rep", "mp", None),
        P("mp", None),
        P("mp", "rep", None),
        P("mp", "rep", None),
    )
    out_specs = (P("rep", "mp", None), P("mp", "rep", None), P("mp", "rep", None))
    return jax.shard_map(
        on_device, mesh=mesh, in_specs=in_specs, out_specs=out_specs, check_vma=False
    )
```

profile of v0, /device:TPU:1, one launch (start us, length us, event | category | flops | bytes accessed | tf_op | source)
XLA Modules:
  0.0 1219.7 jit_solution(4594214810071186189)
XLA Ops:
  7.2 0.0 copy-start
  7.2 0.0 all-reduce.7.cloned.1.call-start
  7.2 0.7 convert_element_type.10
  7.9 1.2 fusion
  9.2 20.2 %psum.49 = f32[256]{0:T(256)S(1)} all-reduce(f32[256]{0:T(256)S(1)} %fusion), channel_id=1, replica_groups=mesh['rep'=64,'mp'=8] {'mp'}, use_global_device_ids=true, to_apply=%region_1.0 | all-reduce | flops 256 | bytes 2048 | tf_op jit(solution)/shard_map/psum | solution.py:47
  29.4 18.6 %all_gather.3 = f32[512,128]{1,0:T(8,128)S(1)} all-gather(f32[64,128]{1,0:T(8,128)} %param.14), channel_id=1, replica_groups=mesh['rep'=64,'mp'=8] {'mp'}, dimensions={0}, use_global_device_ids=true | all-gather | bytes 294912 | tf_op jit(solution)/shard_map/all_gather | solution.py:49
  48.1 0.0 copy-done
  48.1 2.3 bitcast_add_fusion
  50.4 2.6 fusion.42
  53.0 0.0 all-reduce.7.cloned.1.call-update
  53.0 0.0 all-reduce.9.cloned.1.call-start
  53.1 200.2 %all-reduce.7.cloned.1.call-done = f32[1024,128]{1,0:T(8,128)} async-done(((f32[1024,128]{1,0:T(8,128)}), f32[1024,128]{1,0:T(8,128)}) %all-reduce.7.cloned.1.call-update) | async-done | bytes 524304 | tf_op jit(solution)/shard_map/psum | solution.py:59
  253.3 2.8 fusion.14
  256.1 0.0 all-reduce.9.cloned.1.call-update
  256.1 0.2 all-reduce.11.cloned.1.call-start
  256.4 72.7 %all-reduce.9.cloned.1.call-done = f32[128,128]{0,1:T(8,128)} async-done(((f32[128,128]{0,1:T(8,128)}), f32[128,128]{0,1:T(8,128)}) %all-reduce.9.cloned.1.call-update) | async-done | bytes 65552 | tf_op jit(solution)/shard_map/psum | solution.py:60
  329.1 0.9 copy.11
  330.0 0.9 fusion.31
  330.9 11.7 cholesky.44
  342.6 0.6 compare_reduce_fusion.1
  343.3 0.7 fusion.26
  343.9 9.8 custom-call.6
  353.7 1.7 fusion.6
  355.4 4.1 fusion.43
  359.5 0.0 all-reduce.11.cloned.1.call-update
  359.6 0.0 all-reduce.13.cloned.1.call-start
  359.6 274.3 %all-reduce.11.cloned.1.call-done = f32[512,128]{1,0:T(8,128)} async-done(((f32[512,128]{1,0:T(8,128)}), f32[512,128]{1,0:T(8,128)}) %all-reduce.11.cloned.1.call-update) | async-done | bytes 262160 | tf_op jit(solution)/shard_map/psum | solution.py:63
  633.9 3.5 fusion.18
  637.4 0.0 all-reduce.13.cloned.1.call-update
  637.5 0.0 all-reduce.15.cloned.1.call-start
  637.5 189.5 %all-reduce.13.cloned.1.call-done = f32[1024,128]{1,0:T(8,128)} async-done(((f32[1024,128]{1,0:T(8,128)}), f32[1024,128]{1,0:T(8,128)}) %all-reduce.13.cloned.1.call-update) | async-done | bytes 524304 | tf_op jit(solution)/shard_map/psum | solution.py:59
  827.0 2.8 fusion.11
  829.8 0.0 all-reduce.15.cloned.1.call-update
  829.8 0.3 all-reduce.17.cloned.1.call-start
  830.1 72.7 %all-reduce.15.cloned.1.call-done = f32[128,128]{0,1:T(8,128)} async-done(((f32[128,128]{0,1:T(8,128)}), f32[128,128]{0,1:T(8,128)}) %all-reduce.15.cloned.1.call-update) | async-done | bytes 65552 | tf_op jit(solution)/shard_map/psum | solution.py:60
  902.8 0.9 copy.13
  903.7 0.9 fusion.29
  904.5 11.7 cholesky.55
  916.3 0.6 compare_reduce_fusion
  916.9 0.7 fusion.27
  917.6 9.8 custom-call.7
  927.4 1.7 fusion.4
  929.1 4.1 fusion.44
  933.2 0.0 all-reduce.17.cloned.1.call-update
  933.2 274.3 %all-reduce.17.cloned.1.call-done = f32[512,128]{1,0:T(8,128)} async-done(((f32[512,128]{1,0:T(8,128)}), f32[512,128]{1,0:T(8,128)}) %all-reduce.17.cloned.1.call-update) | async-done | bytes 262160 | tf_op jit(solution)/shard_map/psum | solution.py:63
  1207.6 2.8 fusion.16
  1210.4 0.0 copy-start.1
  1210.4 0.0 copy-start.2
  1210.4 1.8 subtract_bitcast_fusion
  1212.2 0.0 copy-done.1
  1212.2 0.0 copy-done.2
  1212.2 0.6 fusion.35
  (3 shorter events, 0.1 us)
Async XLA Ops:
  7.2 40.9 %copy-start = (bf16[256,512]{1,0:T(8,128)(2,1)S(1)}, bf16[256,512]{1,0:T(8,128)(2,1)}, u32[]{:S(2)}) copy-start(bf16[256,512]{1,0:T(8,128)(2,1)} %param.12) | copy-start | bytes 786436
  7.2 246.1 %all-reduce.7.cloned.1.call-start = ((), (), s32[]{:S(2)}) async-start(), calls=%async_computation | async-start | bytes 1048576 | tf_op jit(solution)/shard_map/psum | solution.py:59
  53.0 276.1 %all-reduce.9.cloned.1.call-start = ((), (), s32[]{:S(2)}) async-start(), calls=%async_computation.1 | async-start | bytes 131072 | tf_op jit(solution)/shard_map/psum | solution.py:60
  256.1 377.7 %all-reduce.11.cloned.1.call-start = ((), (), s32[]{:S(2)}) async-start(), calls=%async_computation.2 | async-start | bytes 524288 | tf_op jit(solution)/shard_map/psum | solution.py:63
  359.6 467.4 %all-reduce.13.cloned.1.call-start = ((), (), s32[]{:S(2)}) async-start(), calls=%async_computation.3 | async-start | bytes 1048576 | tf_op jit(solution)/shard_map/psum | solution.py:59
  637.5 265.3 %all-reduce.15.cloned.1.call-start = ((), (), s32[]{:S(2)}) async-start(), calls=%async_computation.4 | async-start | bytes 131072 | tf_op jit(solution)/shard_map/psum | solution.py:60
  829.8 377.7 %all-reduce.17.cloned.1.call-start = ((), (), s32[]{:S(2)}) async-start(), calls=%async_computation.5 | async-start | bytes 524288 | tf_op jit(solution)/shard_map/psum | solution.py:63
  1210.4 1.8 copy-start.1
  1210.4 1.8 copy-start.2
Sparse Core Ops, SparseCore 0:
  53.1 200.1 all-reduce.6
  256.3 72.7 all-reduce.8
  359.7 274.1 all-reduce.10
  637.8 189.1 all-reduce.12
  829.9 72.7 all-reduce.14
  933.4 274.1 all-reduce.16
where the time goes:
time: 1220 us
  waiting for transfers between devices  1080 us (89%)
  other arithmetic  51.8 us (4%)
  blocking collectives  38.9 us (3%)
  matrix products  28.5 us (2%)
  between operations  14.2 us (1%)
    psum x2, waiting for transfers between devices, on_device(): lax.psum(inner_product(merged, orthonormal), ('rep', 'mp')) / replicas  549 us
    psum x2, waiting for transfers between devices, on_device(): left_factor = lax.psum(product(merged, right_factor), 'rep') / replicas  390 us
    psum x2, waiting for transfers between devices, on_device(): gram_matrix = lax.psum(inner_product(left_factor, left_factor), 'mp')  145 us
    another operation x6, other arithmetic, on_device(): lower_factor = jnp.linalg.cholesky(gram_matrix)  24.8 us
  transfers between devices with their start and end apart: 6, of which 6 were waited for; matrix products, arithmetic and copies ran while one was open for 0% of the time, Pallas kernels for 0%

commit v1 on v0

v1 whole, which is shorter than its diff:
```python
import functools

import jax
import jax.numpy as jnp
from jax import lax
from jax.experimental import pallas as pl
from jax.experimental.pallas import tpu as pltpu
from jax.sharding import PartitionSpec as P

D = 8192
CORES = 2
SHAPE = (4, 8)
MESH = pl.DeviceIdType.MESH
F32 = jnp.float32
HI = lax.Precision.HIGHEST
EPS = 1e-5
MOMENTUM = 0.9
RATE = 0.7


def dot(a, b, dims, precision=HI):
    return lax.dot_general(a, b, (dims, ((), ())), precision=precision, preferred_element_type=F32)


NN = ((1,), (0,))
TN = ((0,), (0,))
NT = ((1,), (1,))


def exchange_kernel(
    nx, ny, nz,
    tok_h, gain_ref, kg_h, err_h, basis_ref,
    merged_h, mean_ref, gram_ref, full_ref,
    tok, kg, err, nrm, mg, cx, hs,
    sq, m0a, m0b, m1a, m1b, part, rows, gh, g0a, g0b, g1a, g1b, gpart, gz,
    local_sem, ssem, rsem,
):
    me = lax.axis_index("rep")
    z = lax.axis_index("mp")
    core = lax.rem(me, 2)
    y = lax.rem(lax.div(me, 2), ny)
    x = lax.div(me, 2 * ny)
    reps = nx * ny * CORES
    dl, kw = mg.shape
    half = dl // 2
    ghalf = kw // 2

    def at(xx, yy, cc, zz):
        return ((xx * ny + yy) * 2 + cc, zz)

    partner = at(x, y, 1 - core, z)
    xs = [None] + [at(lax.rem(x + d, nx), y, core, z) for d in range(1, nx)]
    ys = [None] + [at(x, lax.rem(y + d, ny), core, z) for d in range(1, ny)]
    zs = [None] + [at(x, y, core, lax.rem(z + d, nz)) for d in range(1, nz)]

    loads = [
        pltpu.make_async_copy(tok_h, tok, local_sem.at[0]),
        pltpu.make_async_copy(kg_h, kg, local_sem.at[1]),
        pltpu.make_async_copy(err_h.at[0], err, local_sem.at[2]),
    ]
    for load in loads:
        load.start()
    barrier = pltpu.get_barrier_semaphore()
    peers = [partner] + xs[1:] + ys[1:] + zs[1:]
    for peer in peers:
        pl.semaphore_signal(barrier, inc=1, device_id=peer, device_id_type=MESH)

    count = [0]

    def ids(n):
        first = count[0]
        count[0] += n
        return first

    def copy(src, dst, k, dev):
        return pltpu.make_async_remote_copy(
            src_ref=src, dst_ref=dst, send_sem=ssem.at[k], recv_sem=rsem.at[k], device_id=dev, device_id_type=MESH
        )

    def start(copies):
        for c in copies:
            c.start()

    def arrive(copies):
        for c in copies:
            c.wait_recv()

    def sent(copies):
        for c in copies:
            c.wait_send()

    loads[0].wait()
    acc = jnp.zeros((tok.shape[0], 128), F32)
    for b in range(dl // 128):
        t = tok[:, b * 128:(b + 1) * 128].astype(F32)
        acc = acc + t * t
    sq[0] = jnp.sum(acc.T, axis=0, keepdims=True)
    zb = basis_ref.shape[0]
    full_ref[pl.ds(pl.multiple_of(z * zb, zb), zb), :] = basis_ref[...]
    pl.semaphore_wait(barrier, len(peers))

    k = ids(nz)
    sq_copies = [copy(sq.at[0], sq.at[d], k + d, zs[d]) for d in range(1, nz)]
    start(sq_copies)
    k = ids(nz)
    mine = full_ref.at[pl.ds(pl.multiple_of(z * zb, zb), zb), :]
    basis_copies = [copy(basis_ref, mine, k + d, zs[d]) for d in range(1, nz)]
    start(basis_copies)
    arrive(sq_copies)
    total = sq[0]
    for d in range(1, nz):
        total = total + sq[d]
    scale = lax.rsqrt(total / D + EPS)
    scale = jnp.broadcast_to(scale, (128, scale.shape[1])).T
    for b in range(dl // 128):
        cols = slice(b * 128, (b + 1) * 128)
        t = tok[:, cols].astype(F32) * scale * gain_ref[:, cols].astype(F32)
        nrm[:, cols] = t.astype(jnp.bfloat16)
    loads[1].wait()
    loads[2].wait()

    step = half // 2
    k = ids(2)
    pair_copies = []

    def merge(first):
        first = pl.multiple_of(first, step)
        w = dot(nrm[:, pl.ds(first, step)], kg[...], TN, None)
        mg[pl.ds(first, step), :] = w + err[pl.ds(first, step), :]

    for i in range(2):
        first = pl.multiple_of((1 - core) * half + i * step, step)
        merge(first)
        c = copy(mg.at[pl.ds(first, step), :], cx.at[pl.ds(i * step, step), :], k + i, partner)
        c.start()
        pair_copies.append(c)
    for i in range(2):
        merge(core * half + i * step)
    store = pltpu.make_async_copy(mg, merged_h, local_sem.at[3])
    store.start()
    for i in range(2):
        pair_copies[i].wait_recv()
        own = pl.ds(pl.multiple_of(core * half + i * step, step), step)
        hs[i * step:(i + 1) * step, :] = mg[own, :] + cx[i * step:(i + 1) * step, :]

    def scatter(src, base, size, slots, peers, place, n, k):
        out = []
        for d in range(1, n):
            target = lax.rem(place + d, n)
            first = pl.multiple_of(base + target * size, size)
            out.append(copy(src.at[pl.ds(first, size), :], slots.at[d], k + d, peers[d]))
        return out

    def gathered(src, base, size, slots, place, n):
        v = src[pl.ds(pl.multiple_of(base + place * size, size), size), :]
        for d in range(1, n):
            v = v + slots[d]
        return v

    big = max(nx, ny)
    ka, kb = ids(big), ids(big)
    rp = half // (nx * ny)
    row = pl.multiple_of(jnp.where(core == 0, (x * ny + y) * rp, half + (y * nx + x) * rp), rp)

    def plane(src, part, a0, b0, a1, b1, piece, ka, kb, put):
        @pl.when(core == 0)
        def _():
            first = scatter(src, 0, ny * piece, a0, xs, x, nx, ka)
            start(first)
            arrive(first)
            part[pl.ds(0, ny * piece), :] = gathered(src, 0, ny * piece, a0, x, nx)
            second = scatter(part, 0, piece, b0, ys, y, ny, kb)
            start(second)
            arrive(second)
            put(gathered(part, 0, piece, b0, y, ny))
            sent(first)
            sent(second)

        @pl.when(core == 1)
        def _():
            first = scatter(src, 0, nx * piece, a1, ys, y, ny, ka)
            start(first)
            arrive(first)
            part[pl.ds(0, nx * piece), :] = gathered(src, 0, nx * piece, a1, y, ny)
            second = scatter(part, 0, piece, b1, xs, x, nx, kb)
            start(second)
            arrive(second)
            put(gathered(part, 0, piece, b1, x, nx))
            sent(first)
            sent(second)

    def put_rows(v):
        v = v * (1.0 / reps)
        mean_ref[pl.ds(row, rp), :] = v
        rows[0] = v

    plane(hs, part, m0a, m0b, m1a, m1b, rp, ka, kb, put_rows)

    k = ids(1)
    row_copy = copy(rows.at[0], rows.at[1], k, partner)
    row_copy.start()

    def spread(ref, base0, base1, piece, ka, kb):
        def block(first, size):
            return ref.at[pl.ds(pl.multiple_of(first, size), size), :]

        def along(first, size, peers, n, k):
            return [copy(block(first, size), block(first, size), k + d, peers[d]) for d in range(1, n)]

        one0 = along(base0 + (x * ny + y) * piece, piece, ys, ny, ka)
        two0 = along(base0 + x * ny * piece, ny * piece, xs, nx, kb)
        one1 = along(base1 + (y * nx + x) * piece, piece, xs, nx, ka)
        two1 = along(base1 + y * nx * piece, nx * piece, ys, ny, kb)
        return one0, two0, one1, two1

    def by_core(zero, one, act):
        @pl.when(core == 0)
        def _():
            act(zero)

        @pl.when(core == 1)
        def _():
            act(one)

    mean_one0, mean_two0, mean_one1, mean_two1 = spread(mean_ref, 0, half, rp, ids(big), ids(big))
    by_core(mean_one0, mean_one1, start)

    row_copy.wait_recv()
    both = rows[...].reshape(2 * rp, kw)
    lhs = rows[:, :, pl.ds(pl.multiple_of(core * ghalf, ghalf), ghalf)].reshape(2 * rp, ghalf)
    gh[...] = dot(lhs, both, TN)
    gp = ghalf // (nx * ny)
    grow = pl.multiple_of(jnp.where(core == 0, (x * ny + y) * gp, ghalf + (y * nx + x) * gp), gp)

    def put_gram(v):
        gz[0] = v

    plane(gh, gpart, g0a, g0b, g1a, g1b, gp, ids(big), ids(big), put_gram)
    k = ids(nz)
    z_copies = [copy(gz.at[0], gz.at[d], k + d, zs[d]) for d in range(1, nz)]
    start(z_copies)
    by_core(mean_one0, mean_one1, arrive)
    by_core(mean_two0, mean_two1, start)
    arrive(z_copies)
    v = gz[0]
    for d in range(1, nz):
        v = v + gz[d]
    gram_ref[pl.ds(grow, gp), :] = v

    gram_one0, gram_two0, gram_one1, gram_two1 = spread(gram_ref, 0, ghalf, gp, ids(big), ids(big))
    by_core(gram_one0, gram_one1, start)
    by_core(gram_one0, gram_one1, arrive)
    by_core(gram_two0, gram_two1, start)
    by_core(gram_two0, gram_two1, arrive)

    def swap(ref, size, k):
        own = ref.at[pl.ds(pl.multiple_of(core * size, size), size), :]
        return copy(own, own, k, partner)

    gram_swap = swap(gram_ref, ghalf, ids(1))
    gram_swap.start()
    by_core(mean_two0, mean_two1, arrive)
    mean_swap = swap(mean_ref, half, ids(1))
    mean_swap.start()
    arrive(basis_copies)
    gram_swap.wait_recv()
    mean_swap.wait_recv()
    store.wait()
    sent(sq_copies + basis_copies + pair_copies + [row_copy] + z_copies + [gram_swap, mean_swap])
    by_core(mean_one0, mean_one1, sent)
    by_core(mean_two0, mean_two1, sent)
    by_core(gram_one0, gram_one1, sent)
    by_core(gram_two0, gram_two1, sent)


def inverse_factor(a):
    n = a.shape[0]
    groups = n // 8
    left = [a[8 * g:8 * g + 8, :] for g in range(groups)]
    row_id = lax.broadcasted_iota(jnp.int32, (8, n), 0)
    lane_id = lax.broadcasted_iota(jnp.int32, (8, n), 1)
    right = [jnp.where(lane_id == row_id + 8 * g, 1.0, 0.0).astype(F32) for g in range(groups)]
    done = list(right)
    for j in range(n):
        g, i = divmod(j, 8)
        pivot_row = jnp.broadcast_to(left[g][i:i + 1, :], (8, n))
        pivot = jnp.broadcast_to(pivot_row[:, j:j + 1], (8, n))
        inv = 1.0 / pivot
        unit = jnp.broadcast_to(right[g][i:i + 1, :], (8, n))
        done[g] = jnp.where(row_id == i, unit * lax.rsqrt(pivot), done[g])
        pivot_row = pivot_row * inv
        unit = unit * inv
        for h in range(g, groups):
            factor = jnp.broadcast_to(left[h][:, j:j + 1], (8, n))
            if h == g:
                factor = jnp.where(row_id > i, factor, 0.0)
            left[h] = left[h] - factor * pivot_row
            right[h] = right[h] - factor * unit
    return jnp.concatenate(done, axis=0)


def local_kernel(
    rows_each, merged_ref, mean_ref, gram_ref, full_ref, weights_ref, momentum_ref,
    error_out, weights_out, momentum_out, own_ref,
):
    me = lax.axis_index("rep")
    gram = gram_ref[...]
    first = full_ref[...]
    reached = dot(gram, first, NN)
    lower_inv = inverse_factor(dot(first, reached, TN))
    right = dot(reached, lower_inv, NT)
    reached = dot(gram, right, NN)
    lower_inv = inverse_factor(dot(right, reached, TN))
    to_left = dot(right, lower_inv, NT)
    right = dot(reached, lower_inv, NT)
    left = dot(mean_ref[...], to_left, NN)
    own_ref[...] = left
    error_out[0] = merged_ref[...] - dot(left, right, NT)
    mine = own_ref[pl.ds(pl.multiple_of(me * rows_each, rows_each), rows_each), :]
    approx = dot(mine, right, NT)
    momentum = MOMENTUM * momentum_ref[0] + approx
    momentum_out[0] = momentum
    weights_out[0] = weights_ref[0] - RATE * (approx + MOMENTUM * momentum)


def on_device(nx, ny, nz, tokens_in, norm_gain, key_grad, error_in, basis_init, weights_in, momentum_in):
    tok, dl = tokens_in.shape
    kw = key_grad.shape[1]
    rank = basis_init.shape[1]
    half, ghalf = dl // 2, kw // 2
    rp, gp = half // (nx * ny), ghalf // (nx * ny)
    vmem = pl.BlockSpec(memory_space=pltpu.VMEM)
    anywhere = pl.BlockSpec(memory_space=pl.ANY)
    big = max(nx, ny)
    copies = 3 * nz + 2 + 2 * big + 1 + 2 * big + 2 * big + 2 * big + 2
    V = pltpu.VMEM
    merged, mean, gram, full = pl.pallas_call(
        functools.partial(exchange_kernel, nx, ny, nz),
        out_shape=[
            jax.ShapeDtypeStruct((dl, kw), F32),
            jax.ShapeDtypeStruct((dl, kw), F32),
            jax.ShapeDtypeStruct((kw, kw), F32),
            jax.ShapeDtypeStruct((kw, rank), F32),
        ],
        in_specs=[anywhere, vmem, anywhere, anywhere, vmem],
        out_specs=[anywhere, vmem, vmem, vmem],
        scratch_shapes=[
            V((tok, dl), jnp.bfloat16),
            V((tok, kw), jnp.bfloat16),
            V((dl, kw), F32),
            V((tok, dl), jnp.bfloat16),
            V((dl, kw), F32),
            V((half, kw), F32),
            V((half, kw), F32),
            V((nz, 1, tok), F32),
            V((nx, ny * rp, kw), F32),
            V((ny, rp, kw), F32),
            V((ny, nx * rp, kw), F32),
            V((nx, rp, kw), F32),
            V((big * rp, kw), F32),
            V((2, rp, kw), F32),
            V((ghalf, kw), F32),
            V((nx, ny * gp, kw), F32),
            V((ny, gp, kw), F32),
            V((ny, nx * gp, kw), F32),
            V((nx, gp, kw), F32),
            V((big * gp, kw), F32),
            V((nz, gp, kw), F32),
            pltpu.SemaphoreType.DMA((4,)),
            pltpu.SemaphoreType.DMA((copies,)),
            pltpu.SemaphoreType.DMA((copies,)),
        ],
        compiler_params=pltpu.CompilerParams(
            collective_id=0, has_side_effects=True, vmem_limit_bytes=48 * 1024 * 1024
        ),
        name="exchange",
    )(tokens_in, norm_gain.reshape(1, dl), key_grad, error_in, basis_init)
    rows_each = weights_in.shape[1]
    return pl.pallas_call(
        functools.partial(local_kernel, rows_each),
        out_shape=[
            jax.ShapeDtypeStruct((1, dl, kw), F32),
            jax.ShapeDtypeStruct(weights_in.shape, F32),
            jax.ShapeDtypeStruct(momentum_in.shape, F32),
        ],
        in_specs=[vmem] * 6,
        out_specs=[vmem] * 3,
        scratch_shapes=[V((dl, rank), F32)],
        compiler_params=pltpu.CompilerParams(vmem_limit_bytes=48 * 1024 * 1024),
        name="local",
    )(merged, mean, gram, full, weights_in, momentum_in)


def solution(mesh):
    nz = mesh.shape["mp"]
    nx, ny = SHAPE if mesh.shape["rep"] == 64 else (2, mesh.shape["rep"] // 4)
    in_specs = (
        P("rep", "mp"),
        P("mp"),
        P("rep", None),
        P("rep", "mp", None),
        P("mp", None),
        P("mp", "rep", None),
        P("mp", "rep", None),
    )
    out_specs = (P("rep", "mp", None), P("mp", "rep", None), P("mp", "rep", None))
    return jax.shard_map(
        functools.partial(on_device, nx, ny, nz),
        mesh=mesh, in_specs=in_specs, out_specs=out_specs, check_vma=False,
    )
```

time: 1220 us -> 140 us (0.11)
  waiting for transfers between devices: 1080 us -> 0 us
  Pallas kernels: 0 us -> 134 us
  other arithmetic: 51.8 us -> 0 us
  blocking collectives: 38.9 us -> 0 us
  matrix products: 28.5 us -> 0 us
  between operations: 14.2 us -> 0.67 us
    psum x6 -> x0, waiting for transfers between devices: 1080 us -> none  [the longest x2 549 us: on_device(): lax.psum(inner_product(merged, orthonormal), ('rep', 'mp')) / replicas]
    pallas_call x0 -> x2, Pallas kernels: none -> 134 us  [the longest x1 86.1 us: on_device(): pl.pallas_call(functools.partial(exchange_kernel, nx, ny, nz), out_shape=...]
    another operation x10 -> x0, other arithmetic: 45.7 us -> none  [the longest x6 24.8 us: on_device(): lower_factor = jnp.linalg.cholesky(gram_matrix)]
    dot_general x8 -> x0, matrix products: 25.2 us -> none  [the longest x4 13.9 us: inner_product(): lax.dot_general(first, second, (((0,), (0,)), ((), ())), precision=precis...]
    psum x1 -> x0, blocking collectives: 20.2 us -> none  [on_device(): square_sums = lax.psum(jnp.sum(widened * widened, axis=1), 'mp')]
    all_gather x1 -> x0, blocking collectives: 18.6 us -> none  [on_device(): right_factor = lax.all_gather(basis_init, 'mp', axis=0, tiled=True)]
  transfers between devices with their start and end apart: 6 -> 0, of which waited for: 6 -> 0; matrix products, arithmetic and copies ran while one was open for 0% -> 0% of each run, Pallas kernels for 0% -> 0%
where the time goes in v1:
time: 140 us
  Pallas kernels  134 us (96%)
  local copies, waits for them, and re-layouts  5.03 us (4%)
    pallas_call x1, Pallas kernels, on_device(): pl.pallas_call(functools.partial(exchange_kernel, nx, ny, nz), out_shape=...  86.1 us
    pallas_call x1, Pallas kernels, on_device(): pl.pallas_call(functools.partial(local_kernel, rows_each), out_shape=[jax...  47.8 us
    unnamed x12, local copies, waits for them, and re-layouts  4.34 us

profile of v1, /device:TPU:1, one launch (start us, length us, event | category | flops | bytes accessed | tf_op | source)
XLA Modules:
  0.0 139.6 jit_solution(18089942615680421946)
XLA Ops:
  0.6 0.7 reshape.9.gain_ref
  1.3 0.0 copy-start.1
  1.3 1.0 copy-done.1
  2.4 0.0 copy-start.2
  2.4 0.9 copy-done.2
  3.3 0.0 copy-start.3
  3.3 0.8 copy-done.3
  4.1 0.0 copy-start.4
  4.1 0.0 copy-start.5
  4.1 86.1 %exchange.1 = (f32[1024,512]{1,0:T(8,128)S(1)}, f32[1024,512]{1,0:T(8,128)}, f32[512,512]{1,0:T(8,128)S(1)}, f32[512,128]{1,0:T(8,128)S(1)}) custom-call(bf16[256,1024]{1,0:T(8,128)(2,1)S(1)} %copy-done.1, bf16[1,1024]{1,0:T(2,128)(2,1)S(1)} %reshape.9.gain_ref, bf16[256,512]{1,0:T(8,128)(2,1)S(1)} %copy-done.2, f32[1,1024,512]{2,1,0:T(8,128)} %err_h.1, ...), custom_call_target="tpu_custom_call" | custom-call | tf_op jit(solution)/shard_map/exchange/pallas_call | solution.py:337
  90.2 0.0 copy-done.4
  90.2 0.0 copy-done.5
  90.2 0.0 copy-start
  90.2 1.6 %copy-done = f32[1024,512]{1,0:T(8,128)S(1)} copy-done((f32[1024,512]{1,0:T(8,128)S(1)}, f32[1024,512]{1,0:T(8,128)}, u32[]{:S(2)}) %copy-start) | copy-done | bytes 2097176
  91.8 47.8 %local.1 = (f32[1,1024,512]{2,1,0:T(8,128)}, f32[1,16,512]{2,1,0:T(8,128)}, f32[1,16,512]{2,1,0:T(8,128)}) custom-call(f32[1024,512]{1,0:T(8,128)S(1)} %get-tuple-element.7.merged_ref, f32[1024,512]{1,0:T(8,128)S(1)} %copy-done, f32[512,512]{1,0:T(8,128)S(1)} %get-tuple-element.9.gram_ref, f32[512,128]{1,0:T(8,128)S(1)} %get-tuple-element.10.full_ref, ...), custom_call_target="tpu_custom_call" | custom-call | tf_op jit(solution)/shard_map/local/pallas_call | solution.py:379
Async XLA Ops:
  1.3 1.0 copy-start.1
  2.4 0.9 copy-start.2
  3.3 0.8 copy-start.3
  4.1 86.1 %copy-start.4 = (f32[1,16,512]{2,1,0:T(8,128)S(1)}, f32[1,16,512]{2,1,0:T(8,128)}, u32[]{:S(2)}) copy-start(f32[1,16,512]{2,1,0:T(8,128)} %weights_ref.1) | copy-start | bytes 98308
  4.1 86.2 %copy-start.5 = (f32[1,16,512]{2,1,0:T(8,128)S(1)}, f32[1,16,512]{2,1,0:T(8,128)}, u32[]{:S(2)}) copy-start(f32[1,16,512]{2,1,0:T(8,128)} %momentum_ref.1) | copy-start | bytes 98308
  90.2 1.6 %copy-start = (f32[1024,512]{1,0:T(8,128)S(1)}, f32[1024,512]{1,0:T(8,128)}, u32[]{:S(2)}) copy-start(f32[1024,512]{1,0:T(8,128)} %get-tuple-element.8.mean_ref) | copy-start | bytes 6291460

commit v2 on v1

v2 whole, which is shorter than its diff:
```python
import functools

import jax
import jax.numpy as jnp
from jax import lax
from jax.experimental import pallas as pl
from jax.experimental.pallas import tpu as pltpu
from jax.sharding import PartitionSpec as P

D = 8192
CORES = 2
SHAPE = (4, 8)
MESH = pl.DeviceIdType.MESH
F32 = jnp.float32
HI = lax.Precision.HIGHEST
EPS = 1e-5
MOMENTUM = 0.9
RATE = 0.7


def dot(a, b, dims, precision=HI):
    return lax.dot_general(a, b, (dims, ((), ())), precision=precision, preferred_element_type=F32)


NN = ((1,), (0,))
TN = ((0,), (0,))
NT = ((1,), (1,))
ITERS = 2
UPPER = ((0, 0), (0, 1), (0, 2), (0, 3), (1, 1), (1, 2), (1, 3), (2, 2), (2, 3), (3, 3))


def split_dot(a, b, dims):
    def parts(v):
        high = v.astype(jnp.bfloat16)
        return high, (v - high.astype(F32)).astype(jnp.bfloat16)

    (ah, al), (bh, bl) = parts(a), parts(b)
    return dot(ah, bh, dims, None) + (dot(ah, bl, dims, None) + dot(al, bh, dims, None))


def exchange_kernel(
    nx, ny, nz,
    tok_h, gain_h, kg_h, err_h, basis_h,
    merged_h, left_ref, right_ref,
    mean_ref, gram_ref, cur, to_left, gain_ref, basis_ref,
    tok, kg, err, nrm, mg, cx, hs,
    sq, m0d, m0u, m0b, m1d, m1u, m1b, part, rows, gtri,
    gh0, g0a, g0b, gpart0, gz0, gh1, g1a, g1b, gpart1, gz1,
    local_sem, ssem, rsem,
):
    me = lax.axis_index("rep")
    z = lax.axis_index("mp")
    core = lax.rem(me, 2)
    y = lax.rem(lax.div(me, 2), ny)
    x = lax.div(me, 2 * ny)
    reps = nx * ny * CORES
    dl, kw = mg.shape
    half = dl // 2

    def at(xx, yy, cc, zz):
        return ((xx * ny + yy) * 2 + cc, zz)

    partner = at(x, y, 1 - core, z)
    xs = [None] + [at(lax.rem(x + d, nx), y, core, z) for d in range(1, nx)]
    ys = [None] + [at(x, lax.rem(y + d, ny), core, z) for d in range(1, ny)]
    zs = [None] + [at(x, y, core, lax.rem(z + d, nz)) for d in range(1, nz)]

    loads = [
        pltpu.make_async_copy(tok_h, tok, local_sem.at[0]),
        pltpu.make_async_copy(kg_h, kg, local_sem.at[1]),
        pltpu.make_async_copy(err_h.at[0], err, local_sem.at[2]),
        pltpu.make_async_copy(gain_h, gain_ref, local_sem.at[4]),
        pltpu.make_async_copy(basis_h, basis_ref, local_sem.at[5]),
    ]
    for load in loads:
        load.start()
    barrier = pltpu.get_barrier_semaphore()
    peers = [partner] + xs[1:] + ys[1:] + zs[1:]
    for peer in peers:
        pl.semaphore_signal(barrier, inc=1, device_id=peer, device_id_type=MESH)

    count = [0]

    def ids(n):
        first = count[0]
        count[0] += n
        return first

    def copy(src, dst, k, dev):
        return pltpu.make_async_remote_copy(
            src_ref=src, dst_ref=dst, send_sem=ssem.at[k], recv_sem=rsem.at[k], device_id=dev, device_id_type=MESH
        )

    def start(copies):
        for c in copies:
            c.start()

    def arrive(copies):
        for c in copies:
            c.wait_recv()

    def sent(copies):
        for c in copies:
            c.wait_send()

    loads[0].wait()
    acc = jnp.zeros((tok.shape[0], 128), F32)
    for b in range(dl // 128):
        t = tok[:, b * 128:(b + 1) * 128].astype(F32)
        acc = acc + t * t
    sq[0] = jnp.sum(acc.T, axis=0, keepdims=True)
    zb = basis_ref.shape[0]
    loads[4].wait()
    mine = cur.at[pl.ds(pl.multiple_of(z * zb, zb), zb), :]
    mine[...] = basis_ref[...]
    pl.semaphore_wait(barrier, len(peers))

    k = ids(nz)
    sq_copies = [copy(sq.at[0], sq.at[d], k + d, zs[d]) for d in range(1, nz)]
    start(sq_copies)
    arrive(sq_copies)
    total = sq[0]
    for d in range(1, nz):
        total = total + sq[d]
    scale = lax.rsqrt(total / D + EPS)
    scale = jnp.broadcast_to(scale, (128, scale.shape[1])).T
    loads[3].wait()
    for b in range(dl // 128):
        cols = slice(b * 128, (b + 1) * 128)
        t = tok[:, cols].astype(F32) * scale * gain_ref[:, cols].astype(F32)
        nrm[:, cols] = t.astype(jnp.bfloat16)
    loads[1].wait()
    loads[2].wait()

    step = half // 4
    k = ids(4)
    pair_copies = []
    turn_x, turn_y = x, lax.div(y * 4, ny)

    def quarter(owner, m):
        turn = jnp.where(owner == 0, turn_x, turn_y)
        return pl.multiple_of(lax.rem(turn + (2, 1, 3, 0)[m], 4) * step, step)

    def merge(first):
        first = pl.multiple_of(first, step)
        w = dot(nrm[:, pl.ds(first, step)], kg[...], TN, None)
        mg[pl.ds(first, step), :] = w + err[pl.ds(first, step), :]

    for m in range(4):
        low = quarter(1 - core, m)
        first = pl.multiple_of((1 - core) * half + low, step)
        merge(first)
        c = copy(mg.at[pl.ds(first, step), :], cx.at[pl.ds(low, step), :], k + m, partner)
        c.start()
        pair_copies.append(c)
    for m in range(4):
        merge(core * half + quarter(core, m))

    def ready(m):
        low = quarter(core, m)
        pair_copies[m].wait_recv()
        own = pl.ds(pl.multiple_of(core * half + low, step), step)
        hs[pl.ds(low, step), :] = mg[own, :] + cx[pl.ds(low, step), :]

    k = ids(nz)
    basis_copies = [copy(basis_ref, mine, k + d, zs[d]) for d in range(1, nz)]
    start(basis_copies)
    store = pltpu.make_async_copy(mg, merged_h, local_sem.at[3])
    store.start()
    def scatter(src, base, size, slots, peers, place, n, k):
        out = []
        for d in range(1, n):
            target = lax.rem(place + d, n)
            first = pl.multiple_of(base + target * size, size)
            out.append(copy(src.at[pl.ds(first, size), :], slots.at[d], k + d, peers[d]))
        return out

    def gathered(src, base, size, slots, place, n):
        v = src[pl.ds(pl.multiple_of(base + place * size, size), size), :]
        for d in range(1, n):
            v = v + slots[d]
        return v

    big = max(nx, ny)
    ka, kb = ids((big + 2) * 4), ids(big)
    rp = half // (nx * ny)
    row = pl.multiple_of(jnp.where(core == 0, (x * ny + y) * rp, half + (y * nx + x) * rp), rp)

    def ring(src, size, subs, down, up, low, high, place, n, k, needs):
        hops = n // 2
        sub = size // subs

        def own(t, q):
            first = lax.rem(t + 2 * n, n) * size + q * sub
            return pl.ds(pl.multiple_of(first, sub), sub)

        moved = {}
        for s in range(1, hops + 1):
            for m in needs.get(s, ()):
                ready(m)
            for q in range(subs):
                piece = pl.ds(q * sub, sub)
                sides = [(0, down, low, place - (hops - s + 1))]
                if s < hops:
                    sides.append((1, up, high, place + hops - s))
                for side, slots, peer, t in sides:
                    if s == 1:
                        source = src.at[own(t, q), :]
                    else:
                        moved[side, s - 1, q].wait_recv()
                        source = slots.at[s - 1, piece, :]
                        slots[s - 1, piece, :] = slots[s - 1, piece, :] + src[own(t, q), :]
                    c = copy(source, slots.at[s, piece, :], k + (s * 2 + side) * subs + q, peer)
                    c.start()
                    moved[side, s, q] = c
        last = (src[pl.ds(pl.multiple_of(place * size, size), size), :],)
        for q in range(subs):
            moved[0, hops, q].wait_recv()
            moved[1, hops - 1, q].wait_recv()
        total = last[0] + down[hops] + up[hops - 1]
        return total, list(moved.values())

    def plane(src, part, slots0, slots1, b0, b1, piece, subs, ka, kb, put):
        @pl.when(core == 0)
        def _():
            total, first = ring(src, ny * piece, subs, slots0[0], slots0[1], xs[nx - 1], xs[1], x, nx, ka, {1: (0, 1), 2: (2, 3)})
            part[pl.ds(0, ny * piece), :] = total
            second = scatter(part, 0, piece, b0, ys, y, ny, kb)
            start(second)
            arrive(second)
            put(gathered(part, 0, piece, b0, y, ny))
            sent(first)
            sent(second)

        @pl.when(core == 1)
        def _():
            total, first = ring(src, nx * piece, subs, slots1[0], slots1[1], ys[ny - 1], ys[1], y, ny, ka, {1: (0, 1), 2: (2,), 3: (3,)})
            part[pl.ds(0, nx * piece), :] = total
            second = scatter(part, 0, piece, b1, xs, x, nx, kb)
            start(second)
            arrive(second)
            put(gathered(part, 0, piece, b1, x, nx))
            sent(first)
            sent(second)

    def put_rows(v):
        v = v * (1.0 / reps)
        mean_ref[pl.ds(row, rp), :] = v
        rows[0] = v

    plane(hs, part, (m0d, m0u), (m1d, m1u), m0b, m1b, rp, 4, ka, kb, put_rows)

    k = ids(1)
    row_copy = copy(rows.at[0], rows.at[1], k, partner)
    row_copy.start()

    def spread(ref, base0, base1, piece, ka, kb):
        def block(first, size):
            return ref.at[pl.ds(pl.multiple_of(first, size), size), :]

        def along(first, size, peers, n, k):
            if first is None:
                return []
            return [copy(block(first, size), block(first, size), k + d, peers[d]) for d in range(1, n)]

        def place(base, index):
            return None if base is None else base + index * piece

        one0 = along(place(base0, x * ny + y), piece, ys, ny, ka)
        two0 = along(place(base0, x * ny), ny * piece, xs, nx, kb)
        one1 = along(place(base1, y * nx + x), piece, xs, nx, ka)
        two1 = along(place(base1, y * nx), nx * piece, ys, ny, kb)
        return one0, two0, one1, two1

    def by_core(zero, one, act):
        @pl.when(core == 0)
        def _():
            act(zero)

        @pl.when(core == 1)
        def _():
            act(one)

    mean_one0, mean_two0, mean_one1, mean_two1 = spread(mean_ref, 0, half, rp, ids(big), ids(big))
    by_core(mean_one0, mean_one1, start)

    row_copy.wait_recv()
    both = rows[...].reshape(2 * rp, kw)
    tile = kw // 4
    tiles = [both[:, i * tile:(i + 1) * tile] for i in range(4)]
    gp0, gp1 = 6 * tile // (nx * ny), 4 * tile // (nx * ny)
    gbase1 = 6 * tile

    def direct(src, part, a, b, first, second, piece, ka, kb):
        (peers1, place1, n1), (peers2, place2, n2) = first, second
        one = scatter(src, 0, n2 * piece, a, peers1, place1, n1, ka)
        start(one)
        arrive(one)
        part[...] = gathered(src, 0, n2 * piece, a, place1, n1)
        two = scatter(part, 0, piece, b, peers2, place2, n2, kb)
        start(two)
        arrive(two)
        v = gathered(part, 0, piece, b, place2, n2)
        sent(one)
        sent(two)
        return v

    ka, kb = ids(big), ids(big)

    @pl.when(core == 0)
    def _():
        for j, (i, k) in enumerate(UPPER[:6]):
            gh0[j * tile:(j + 1) * tile, :] = dot(tiles[i], tiles[k], TN)
        gz0[0] = direct(gh0, gpart0, g0a, g0b, (xs, x, nx), (ys, y, ny), gp0, ka, kb)

    @pl.when(core == 1)
    def _():
        for j, (i, k) in enumerate(UPPER[6:]):
            gh1[j * tile:(j + 1) * tile, :] = dot(tiles[i], tiles[k], TN)
        gz1[0] = direct(gh1, gpart1, g1a, g1b, (ys, y, ny), (xs, x, nx), gp1, ka, kb)

    k = ids(nz)
    z_zero = [copy(gz0.at[0], gz0.at[d], k + d, zs[d]) for d in range(1, nz)]
    z_one = [copy(gz1.at[0], gz1.at[d], k + d, zs[d]) for d in range(1, nz)]
    by_core(z_zero, z_one, start)
    by_core(mean_one0, mean_one1, arrive)

    def near(copies):
        n = len(copies)
        return [c for i, c in enumerate(copies) if min(i, n - 1 - i) < n // 4 + 1]

    def far(copies):
        close = near(copies)
        return [c for c in copies if all(c is not o for o in close)]

    by_core(near(mean_two0), near(mean_two1), start)
    by_core(z_zero, z_one, arrive)

    def over_z(ref, base, piece, index):
        v = ref[0]
        for d in range(1, nz):
            v = v + ref[d]
        gtri[pl.ds(pl.multiple_of(base + index * piece, 8), piece), :] = v

    @pl.when(core == 0)
    def _():
        over_z(gz0, 0, gp0, x * ny + y)

    @pl.when(core == 1)
    def _():
        over_z(gz1, gbase1, gp1, y * nx + x)

    ka, kb = ids(big), ids(big)
    gram_one0, gram_two0, _, _ = spread(gtri, 0, None, gp0, ka, kb)
    _, _, gram_one1, gram_two1 = spread(gtri, None, gbase1, gp1, ka, kb)
    by_core(gram_one0, gram_one1, start)
    by_core(gram_one0, gram_one1, arrive)
    by_core(gram_two0, gram_two1, start)
    by_core(gram_two0, gram_two1, arrive)
    k = ids(2)
    six, four = gtri.at[pl.ds(0, 6 * tile), :], gtri.at[pl.ds(gbase1, 4 * tile), :]
    swap_zero = [copy(six, six, k, partner)]
    swap_one = [copy(four, four, k + 1, partner)]
    by_core(swap_zero, swap_one, start)
    by_core(far(mean_two0), far(mean_two1), start)
    arrive(basis_copies)
    by_core(swap_one, swap_zero, arrive)
    for j, (i, k) in enumerate(UPPER):
        v = gtri[j * tile:(j + 1) * tile, :]
        gram_ref[i * tile:(i + 1) * tile, k * tile:(k + 1) * tile] = v
        if i != k:
            gram_ref[k * tile:(k + 1) * tile, i * tile:(i + 1) * tile] = v.T

    def iterate(step, carry):
        reached = dot(gram_ref[...], cur[...], NN)
        lower_inv = inverse_factor(dot(cur[...], reached, TN))

        @pl.when(step == ITERS - 1)
        def _():
            to_left[...] = dot(cur[...], lower_inv, NT)

        cur[...] = dot(reached, lower_inv, NT)
        return carry

    lax.fori_loop(0, ITERS, iterate, 0)
    by_core(mean_two0, mean_two1, arrive)
    own = pl.ds(pl.multiple_of(core * half, half), half)
    left_ref[own, :] = split_dot(mean_ref[own, :], to_left[...], NN)
    own = left_ref.at[own, :]
    left_swap = copy(own, own, ids(1), partner)
    left_swap.start()
    right_ref[...] = cur[...]
    store.wait()
    left_swap.wait()
    sent(sq_copies + basis_copies + pair_copies + [row_copy])
    by_core(z_zero, z_one, sent)
    by_core(swap_zero, swap_one, sent)
    by_core(mean_one0, mean_one1, sent)
    by_core(mean_two0, mean_two1, sent)
    by_core(gram_one0, gram_one1, sent)
    by_core(gram_two0, gram_two1, sent)


def lane(v, j):
    return jnp.broadcast_to(v[:, j:j + 1], v.shape)


def row(v, i):
    return jnp.broadcast_to(v[i:i + 1, :], v.shape)


def inverse_factor(a):
    n = a.shape[0]
    groups = n // 8
    rows = [a[8 * g:8 * g + 8, :] for g in range(groups)]
    row_id = lax.broadcasted_iota(jnp.int32, (8, n), 0)
    lane_id = lax.broadcasted_iota(jnp.int32, (8, n), 1)
    here = [row_id == i for i in range(8)]
    result = []
    for g in range(groups):
        block = (lane_id >= 8 * g) & (lane_id < 8 * g + 8)
        unit = jnp.where(lane_id == row_id + 8 * g, 1.0, 0.0).astype(F32)
        columns = [lane(rows[g], 8 * g + i) for i in range(8)]
        top = jnp.where(block, unit, rows[g])
        out = top
        for i in range(8):
            pivot = row(columns[i], i)
            inv = 1.0 / pivot
            coeff = jnp.where(here[i], -1.0, columns[i])

            def eliminate(v):
                return jnp.where(here[i], 0.0, v) - coeff * (row(v, i) * inv)

            out = jnp.where(here[i], top * lax.rsqrt(pivot), out)
            for k in range(i + 1, 8):
                columns[k] = eliminate(columns[k])
            top = eliminate(top)
        result.append(jnp.where(lane_id < 8 * g + 8, out, 0.0))
        tops = [row(top, i) for i in range(8)]
        for h in range(g + 1, groups):
            p = [lane(rows[h], 8 * g + i) * tops[i] for i in range(8)]
            p = ((p[0] + p[1]) + (p[2] + p[3])) + ((p[4] + p[5]) + (p[6] + p[7]))
            rows[h] = jnp.where(block, 0.0, rows[h]) - p
    return jnp.concatenate(result, axis=0)


def output_kernel(
    rows_each, merged_ref, left_ref, right_ref, weights_ref, momentum_ref,
    error_h, weights_out, momentum_out, error, sem,
):
    block = error.shape[1]
    stores = []
    for i in range(error.shape[0]):
        here = slice(i * block, (i + 1) * block)
        error[i] = merged_ref[here, :] - split_dot(left_ref[here, :], right_ref[...], NT)
        stores.append(pltpu.make_async_copy(error.at[i], error_h.at[0, pl.ds(i * block, block), :], sem.at[i]))
        stores[i].start()
    first = lax.axis_index("rep") * rows_each
    approx = split_dot(left_ref[pl.ds(pl.multiple_of(first, rows_each), rows_each), :], right_ref[...], NT)
    momentum = MOMENTUM * momentum_ref[0] + approx
    momentum_out[0] = momentum
    weights_out[0] = weights_ref[0] - RATE * (approx + MOMENTUM * momentum)
    for store in stores:
        store.wait()


def on_device(nx, ny, nz, tokens_in, norm_gain, key_grad, error_in, basis_init, weights_in, momentum_in):
    tok, dl = tokens_in.shape
    kw = key_grad.shape[1]
    rank = basis_init.shape[1]
    half, tile = dl // 2, kw // 4
    rp, gp0, gp1 = half // (nx * ny), 6 * tile // (nx * ny), 4 * tile // (nx * ny)
    vmem = pl.BlockSpec(memory_space=pltpu.VMEM)
    anywhere = pl.BlockSpec(memory_space=pl.ANY)
    big = max(nx, ny)
    copies = 3 * nz + 10 + 4 * (big + 2) + 8 * big
    V = pltpu.VMEM
    keep = lambda v: pltpu.with_memory_space_constraint(v, pltpu.HBM)
    merged, left, right = pl.pallas_call(
        functools.partial(exchange_kernel, nx, ny, nz),
        out_shape=[
            jax.ShapeDtypeStruct((dl, kw), F32),
            jax.ShapeDtypeStruct((dl, rank), F32),
            jax.ShapeDtypeStruct((kw, rank), F32),
        ],
        in_specs=[pl.BlockSpec(memory_space=pltpu.HBM)] * 5,
        out_specs=[anywhere, vmem, vmem],
        scratch_shapes=[
            V((dl, kw), F32),
            V((kw, kw), F32),
            V((kw, rank), F32),
            V((kw, rank), F32),
            V((1, dl), jnp.bfloat16),
            V(basis_init.shape, F32),
            V((tok, dl), jnp.bfloat16),
            V((tok, kw), jnp.bfloat16),
            V((dl, kw), F32),
            V((tok, dl), jnp.bfloat16),
            V((dl, kw), F32),
            V((half, kw), F32),
            V((half, kw), F32),
            V((nz, 1, tok), F32),
            V((nx // 2 + 1, ny * rp, kw), F32),
            V((nx // 2 + 1, ny * rp, kw), F32),
            V((ny, rp, kw), F32),
            V((ny // 2 + 1, nx * rp, kw), F32),
            V((ny // 2 + 1, nx * rp, kw), F32),
            V((nx, rp, kw), F32),
            V((big * rp, kw), F32),
            V((2, rp, kw), F32),
            V((10 * tile, tile), F32),
            V((6 * tile, tile), F32),
            V((nx, ny * gp0, tile), F32),
            V((ny, gp0, tile), F32),
            V((ny * gp0, tile), F32),
            V((nz, gp0, tile), F32),
            V((4 * tile, tile), F32),
            V((ny, nx * gp1, tile), F32),
            V((nx, gp1, tile), F32),
            V((nx * gp1, tile), F32),
            V((nz, gp1, tile), F32),
            pltpu.SemaphoreType.DMA((6,)),
            pltpu.SemaphoreType.DMA((copies,)),
            pltpu.SemaphoreType.DMA((copies,)),
        ],
        compiler_params=pltpu.CompilerParams(
            collective_id=0, has_side_effects=True, vmem_limit_bytes=48 * 1024 * 1024
        ),
        name="exchange",
    )(keep(tokens_in), norm_gain.reshape(1, dl), keep(key_grad), keep(error_in), keep(basis_init))
    rows_each = weights_in.shape[1]
    steps = 8
    return pl.pallas_call(
        functools.partial(output_kernel, rows_each),
        out_shape=[
            jax.ShapeDtypeStruct((1, dl, kw), F32),
            jax.ShapeDtypeStruct(weights_in.shape, F32),
            jax.ShapeDtypeStruct(momentum_in.shape, F32),
        ],
        in_specs=[vmem] * 5,
        out_specs=[anywhere, vmem, vmem],
        scratch_shapes=[V((steps, dl // steps, kw), F32), pltpu.SemaphoreType.DMA((steps,))],
        compiler_params=pltpu.CompilerParams(vmem_limit_bytes=24 * 1024 * 1024),
        name="outputs",
    )(merged, left, right, weights_in, momentum_in)


def solution(mesh):
    nz = mesh.shape["mp"]
    nx, ny = SHAPE if mesh.shape["rep"] == 64 else (2, mesh.shape["rep"] // 4)
    in_specs = (
        P("rep", "mp"),
        P("mp"),
        P("rep", None),
        P("rep", "mp", None),
        P("mp", None),
        P("mp", "rep", None),
        P("mp", "rep", None),
    )
    out_specs = (P("rep", "mp", None), P("mp", "rep", None), P("mp", "rep", None))
    return jax.shard_map(
        functools.partial(on_device, nx, ny, nz),
        mesh=mesh, in_specs=in_specs, out_specs=out_specs, check_vma=False,
    )
```

time: 140 us -> 91.3 us (0.65)
  Pallas kernels: 134 us -> 89.7 us
  local copies, waits for them, and re-layouts: 5.03 us -> 0.71 us
    pallas_call x1, Pallas kernels: 47.8 us -> 2.43 us  [on_device(): pl.pallas_call(functools.partial(output_kernel, rows_each), out_shape=[ja...]
    unnamed x12 -> x4, local copies, waits for them, and re-layouts: 4.34 us -> 0.01 us
where the time goes in v2:
time: 91.3 us; the launch traced here: 91.1 us
  Pallas kernels  89.7 us (98%)
    pallas_call x1, Pallas kernels, on_device(): pl.pallas_call(functools.partial(exchange_kernel, nx, ny, nz), out_shape=...  87.3 us
    pallas_call x1, Pallas kernels, on_device(): pl.pallas_call(functools.partial(output_kernel, rows_each), out_shape=[ja...  2.43 us

profile of v2, /device:TPU:1, one launch (start us, length us, event | category | flops | bytes accessed | tf_op | source)
XLA Modules:
  0.0 91.1 jit_solution(16905096575635009404)
XLA Ops:
  0.6 0.0 copy-start.1
  0.6 0.0 copy-start
  0.7 0.7 reshape.9.gain_h
  1.3 87.3 %exchange.1 = (f32[1024,512]{1,0:T(8,128)S(1)}, f32[1024,128]{1,0:T(8,128)S(1)}, f32[512,128]{1,0:T(8,128)S(1)}) custom-call(bf16[256,1024]{1,0:T(8,128)(2,1)} %tok_h.1, bf16[1,1024]{1,0:T(2,128)(2,1)S(1)} %reshape.9.gain_h, bf16[256,512]{1,0:T(8,128)(2,1)} %kg_h.1, f32[1,1024,512]{2,1,0:T(8,128)} %err_h.1, f32[64,128]{1,0:T(8,128)} %basis_h.1), custom_call_target="tpu_custom_call" | custom-call | tf_op jit(solution)/shard_map/exchange/pallas_call | solution.py:479
  88.6 0.0 copy-done.1
  88.6 0.0 copy-done
  88.6 2.4 %outputs.1 = (f32[1,1024,512]{2,1,0:T(8,128)}, f32[1,16,512]{2,1,0:T(8,128)}, f32[1,16,512]{2,1,0:T(8,128)}) custom-call(f32[1024,512]{1,0:T(8,128)S(1)} %get-tuple-element.6.merged_ref, f32[1024,128]{1,0:T(8,128)S(1)} %get-tuple-element.7.left_ref, f32[512,128]{1,0:T(8,128)S(1)} %get-tuple-element.8.right_ref, f32[1,16,512]{2,1,0:T(8,128)S(1)} %copy-done, ...), custom_call_target="tpu_custom_call" | custom-call | tf_op jit(solution)/shard_map/outputs/pallas_call | solution.py:533
Async XLA Ops:
  0.6 88.0 %copy-start.1 = (f32[1,16,512]{2,1,0:T(8,128)S(1)}, f32[1,16,512]{2,1,0:T(8,128)}, u32[]{:S(2)}) copy-start(f32[1,16,512]{2,1,0:T(8,128)} %momentum_ref.1) | copy-start | bytes 98308
  0.6 88.0 %copy-start = (f32[1,16,512]{2,1,0:T(8,128)S(1)}, f32[1,16,512]{2,1,0:T(8,128)}, u32[]{:S(2)}) copy-start(f32[1,16,512]{2,1,0:T(8,128)} %weights_ref.1) | copy-start | bytes 98308
